TPU v7x, 32 devices: a whole 2x2x4 slice. The times are simulated.
32 devices in a mesh: row: 8 (over y, x, core), col: 4 (over z).
Axes of the slice: x: 2, y: 2, z: 4, core: 2. Of those that a mesh axis runs over, the one named last changes fastest.
Arguments:
- image: bfloat16 [512, 512, 512], P('row', 'col'), may hold values from -6 to 6
- w_local: bfloat16 [3, 3, 512, 128], replicated, may hold values from -0.09375 to 0.09375
- w_cross: bfloat16 [3, 3, 128, 384], replicated, may hold values from -0.1875 to 0.1875
- w_spec: bfloat16 [768, 768], replicated, may hold values from -0.21875 to 0.21875
Outputs:
- result: bfloat16 [512, 512, 512], P('row', 'col')
All inputs are finite; a program needn't handle non-finite values.
Results may differ from a plain program's by a relative error of at most 0.0055.
Values may be sent and summed in bfloat16 or wider, within the bound.
A program may use at most 192 MiB of HBM per device.

v0:
```python
import jax
import jax.numpy as jnp
import numpy as np
from jax import lax
from jax.sharding import PartitionSpec as P

BOTH = ("row", "col")


def rounded(table):
    return np.asarray(table, np.float32).astype(jnp.bfloat16)


def column_table(height):
    freq = np.arange(height // 2)
    angle = 2.0 * np.pi * (np.outer(freq, np.arange(height)) % height) / height
    table = np.stack([np.cos(angle), -np.sin(angle)], axis=1)
    table[0, 1] = 1.0 - 2.0 * (np.arange(height) % 2)
    return rounded(table.reshape(height, height) / np.sqrt(height))


def width_order(nrow, ncol, width):
    part = width // (nrow * ncol)
    r, c, i = np.meshgrid(np.arange(nrow), np.arange(ncol), np.arange(part), indexing="ij")
    return (c * (width // ncol) + r * part + i).reshape(-1)


def width_tables(order, width, padded):
    half = width // 2
    count = width + 2
    plain = np.concatenate([np.arange(width), [0, half]])
    packed = np.concatenate([np.arange(half + 1), np.arange(half + 1)])
    rows = np.arange(count)
    out = []
    for freq in (plain, packed):
        angle = 2.0 * np.pi * (np.outer(freq, order) % width) / width
        pair = np.zeros((2, padded, width))
        pair[0, :count] = np.cos(angle) / np.sqrt(width)
        pair[1, :count] = np.sin(angle) / np.sqrt(width)
        out.append(rounded(pair))
    sign = np.where(rows <= half, 1.0, -1.0)
    scale_plain = np.where(np.isin(rows, [0, half, width, width + 1]), 1.0, 2.0)
    scale_packed = np.where(np.isin(packed, [0, half]), 1.0, 2.0)
    extra = padded - count
    pad = lambda v: np.pad(v, (0, extra))
    upper = pad((rows <= half).astype(np.float64))
    lower = pad((rows > half).astype(np.float64))
    return (out[0], out[1], pad(sign), upper, lower, pad(scale_plain), pad(scale_packed))


def assembled(pair, blocks, xp):
    cosine, sine = (pair[0], pair[1])
    pick = {"c": cosine, "s": sine}
    lines = []
    for line in blocks:
        lines.append(xp.concatenate([pick[k] * v[:, None] for k, v in line], axis=1))
    return xp.concatenate(lines, axis=0)


def extended(cells, sides, width):
    for axis, dim in sides:
        count = lax.axis_size(axis)
        ends = count - 1
        head = lax.slice_in_dim(cells, 0, width, axis=dim)
        tail = lax.slice_in_dim(cells, cells.shape[dim] - width, cells.shape[dim], axis=dim)
        cells = jnp.concatenate(
            [
                lax.ppermute(tail, axis, [(i, (i + 1) % count) for i in range(ends)]),
                cells,
                lax.ppermute(head, axis, [((i + 1) % count, i) for i in range(ends)]),
            ],
            axis=dim,
        )
    return cells


def conv(padded, weight):
    return lax.conv_general_dilated(
        padded[None],
        weight,
        (1, 1),
        "VALID",
        dimension_numbers=("NHWC", "HWIO", "NHWC"),
        preferred_element_type=jnp.float32,
    )[0]


def product(form, left, right):
    return jnp.einsum(form, left, right, preferred_element_type=jnp.float32)


def global_branch(glob, w_spec):
    nrow, ncol = (lax.axis_size("row"), lax.axis_size("col"))
    count = nrow * ncol
    height, width, ch = (glob.shape[0] * nrow, glob.shape[1] * ncol, glob.shape[2])
    bins = height // (2 * count)
    padded = -(-(width + 2) // 16) * 16
    columns = lax.all_to_all(glob, "row", split_axis=1, concat_axis=0, tiled=True)
    col_np = column_table(height)
    plain_np, packed_np, sign, upper, lower, scale_plain, scale_packed = width_tables(
        width_order(nrow, ncol, width), width, padded
    )
    ones = np.ones_like(sign)
    plain_form = ((("c", ones), ("s", ones)), (("s", -sign), ("c", sign)))
    packed_form = ((("c", upper), ("c", lower)), (("s", -upper), ("s", -lower)))

    def row_sums(pair, form, scale):
        table = assembled(pair.astype(np.float64), form, np) * np.tile(scale, 2)[:, None]
        return np.stack([table[:padded].sum(0), table[padded:].sum(0)], axis=1).astype(np.float32)

    def cast_form(form):
        return [[(k, jnp.asarray(rounded(v))) for k, v in line] for line in form]

    col_table = jnp.asarray(col_np)
    is_first = lax.axis_index(BOTH) == 0
    special = (is_first & (jnp.arange(bins) == 0))[:, None, None]
    table = jnp.where(
        special,
        assembled(jnp.asarray(packed_np), cast_form(packed_form), jnp)[None],
        assembled(jnp.asarray(plain_np), cast_form(plain_form), jnp)[None],
    )
    scale = jnp.where(
        special,
        jnp.asarray(scale_packed, jnp.float32)[None, :, None],
        jnp.asarray(scale_plain, jnp.float32)[None, :, None],
    )
    sums = jnp.where(
        special,
        jnp.asarray(row_sums(packed_np, packed_form, scale_packed))[None],
        jnp.asarray(row_sums(plain_np, plain_form, scale_plain))[None],
    )
    field = product("uh,hwc->uwc", col_table, columns).astype(jnp.bfloat16)
    lines = lax.all_to_all(field, BOTH, split_axis=0, concat_axis=1, tiled=True)
    lines = lines.reshape(bins, 2 * width, ch)
    spectrum = product("bmk,bkc->bmc", table, lines).astype(jnp.bfloat16)
    stacked = jnp.concatenate([spectrum[:, :padded], spectrum[:, padded:]], axis=-1)
    mixed = jnp.maximum(product("bvc,co->bvo", stacked, w_spec), 0.0)
    own_sum = jnp.sum(mixed, axis=(0, 1))
    every = lax.all_to_all(
        jnp.broadcast_to(own_sum[None], (count, 2 * ch)),
        BOTH,
        split_axis=0,
        concat_axis=0,
        tiled=True,
    )
    mean = jnp.sum(every, axis=0) / (height * (width // 2 + 1))
    scaled = (mixed * scale).astype(jnp.bfloat16)
    scaled = jnp.concatenate([scaled[..., :ch], scaled[..., ch:]], axis=1)
    offset = sums[:, :, :1] * mean[:ch] + sums[:, :, 1:] * mean[ch:]
    inverted = (product("bkm,bkc->bmc", table, scaled) - offset).astype(jnp.bfloat16)
    inverted = inverted.reshape(2 * bins, width, ch)
    back = lax.all_to_all(inverted, BOTH, split_axis=1, concat_axis=0, tiled=True)
    rows = product("uh,uwc->hwc", col_table, back).astype(jnp.bfloat16)
    return lax.all_to_all(rows, "row", split_axis=0, concat_axis=1, tiled=True)


def body(image, w_local, w_cross, w_spec):
    local_chan = w_cross.shape[2]
    spectral = global_branch(image[..., local_chan:], w_spec)
    padded = extended(image, (("row", 0), ("col", 1)), 1)
    local_out = conv(padded, w_local)
    cross_out = conv(padded[..., :local_chan], w_cross)
    result = jnp.concatenate(
        [local_out.astype(jnp.bfloat16), (cross_out + spectral).astype(jnp.bfloat16)], axis=-1
    )
    return result


def solution(mesh):
    in_specs = (P("row", "col", None), P(), P(), P())
    out_specs = P("row", "col", None)
    return jax.shard_map(body, mesh=mesh, in_specs=in_specs, out_specs=out_specs, check_vma=False)
```

profile of v0, /device:TPU:11, one launch (start us, length us, event | category | flops | bytes accessed | tf_op | source)
XLA Modules:
  0.0 627.0 jit_solution(2966774456978388852)
XLA Ops:
  0.0 11.6 %copy.97 = bf16[64,128,512]{2,0,1:T(8,128)(2,1)} copy(bf16[64,128,512]{2,1,0:T(8,128)(2,1)} %param.19) | data formatting | bytes 16777216 | tf_op args[0]
  11.6 2.8 slice-done
  14.4 74.4 %all_to_all.66 = bf16[64,128,384]{2,0,1:T(8,128)(2,1)S(1)} all-to-all(bf16[64,128,384]{2,0,1:T(8,128)(2,1)S(1)} %slice-done), channel_id=1, replica_groups=mesh['row'=8,'col'=4] {'row'}, dimensions={1} | all-to-all | bytes 12582912 | tf_op jit(solution)/shard_map/all_to_all | solution.py:98
  88.8 3.8 copy.106
  92.6 4.2 fusion.40
  96.8 6.4 %copy.108 = bf16[512,16,384]{2,1,0:T(8,128)(2,1)} copy(bf16[512,16,384]{2,0,1:T(8,128)(2,1)S(1)} %fusion.40) | data formatting | bytes 12582912 | tf_op jit(solution)/shard_map/convert_element_type | solution.py:132
  103.2 5.9 all-to-all-start.1
  109.1 0.0 copy-start.9
  109.2 0.1 broadcast_select_fusion.1
  109.2 0.1 broadcast_select_fusion
  109.3 137.3 %all-to-all-done.1 = bf16[512,16,384]{2,1,0:T(8,128)(2,1)} async-done(((bf16[512,16,384]{2,1,0:T(8,128)(2,1)}), bf16[512,16,384]{2,1,0:T(8,128)(2,1)}, u32[]{:S(2)}, u32[]{:S(2)}) %all-to-all-start.1) | async-done | bytes 6291488 | tf_op jit(solution)/shard_map/all_to_all | solution.py:133
  246.6 3.9 copy.109
  250.5 9.8 %fusion.20 = bf16[8,1056,384]{2,1,0:T(8,128)(2,1)S(1)} fusion(bf16[8,1024,384]{2,1,0:T(8,128)(2,1)S(1)} %bitcast.62, pred[8]{0:T(512)(128)(4,1)S(1)} %compare_and_fusion, bf16[1056,1024]{1,0:T(8,128)(2,1)S(1)} %copy-done.9, bf16[1056,1024]{1,0:T(8,128)(2,1)S(1)} %copy-done.10), kind=kOutput, calls=%fused_computation.28 | convolution fusion | flops 6655672320 | bytes 17104904 | tf_op jit(solution)/shard_map/bmk,bkc->bmc/dot_general | solution.py:89
  260.3 0.7 fusion.65
  261.0 7.1 %maximum_reduce_fusion = (f32[768]{0:T(1024)S(1)}, bf16[8,528,768]{2,1,0:T(8,128)(2,1)}) fusion(f32[8,528]{1,0:T(8,128)S(1)} %broadcast_select_fusion.1, bf16[768,768]{1,0:T(8,128)(2,1)S(1)} %copy-done, bf16[8,528,384]{2,1,0:T(8,128)(2,1)S(1)} %get-tuple-element.14, bf16[8,528,384]{2,1,0:T(8,128)(2,1)S(1)} %get-tuple-element.13), kind=kOutput, calls=%fused_computation.14 | convolution fusion | flops 5008784384 | bytes 14175744 | tf_op jit(solution)/shard_map/bvc,co->bvo/dot_general | solution.py:89
  268.1 0.7 broadcast_in_dim.112
  268.8 6.8 %all-to-all-start.2 = ((f32[32,1,768]{2,1,0:T(1,128)}), f32[32,1,768]{2,1,0:T(1,128)S(1)}, u32[]{:S(2)}, u32[]{:S(2)}) async-start(f32[32,1,768]{2,1,0:T(1,128)} %broadcast_in_dim.112), calls=%async_computation.2 | async-start | bytes 196608 | tf_op jit(solution)/shard_map/all_to_all | solution.py:139
  275.6 6.3 %fusion.64 = (bf16[8,528,384]{2,1,0:T(8,128)(2,1)}, bf16[8,528,384]{2,1,0:T(8,128)(2,1)}) fusion(bf16[8,528,768]{2,1,0:T(8,128)(2,1)} %get-tuple-element.6), kind=kLoop, calls=%fused_computation.73 | loop fusion | bytes 12976128 | tf_op jit(solution)/shard_map/slice | solution.py:148
  281.9 0.0 all-to-all-done.2
  281.9 0.1 reduce_sum.19
  282.0 14.6 %subtract_convert_fusion = bf16[8,1024,384]{2,1,0:T(8,128)(2,1)S(1)} fusion(bf16[8,528,384]{2,1,0:T(8,128)(2,1)} %get-tuple-element.12, bf16[8,528,384]{2,1,0:T(8,128)(2,1)} %get-tuple-element.11, pred[8]{0:T(512)(128)(4,1)S(1)} %compare_and_fusion, bf16[1056,1024]{1,0:T(8,128)(2,1)S(1)} %copy-done.9, bf16[1056,1024]{1,0:T(8,128)(2,1)} %constant.82, ...), kind=kOutput, calls=%fused_computation.13 | convolution fusion | flops 6681133056 | bytes 17173512 | tf_op jit(solution)/shard_map/bkm,bkc->bmc/dot_general | solution.py:89
  296.6 6.4 %copy.111 = bf16[16,512,384]{2,0,1:T(8,128)(2,1)} copy(bf16[16,512,384]{2,1,0:T(8,128)(2,1)S(1)} %bitcast.59) | data formatting | bytes 12582912 | tf_op jit(solution)/shard_map/reshape | solution.py:151
  303.0 5.9 all-to-all-start.3
  308.9 1.0 fusion.63
  309.9 3.4 collective-permute-start
  313.2 1.9 collective-permute-start.1
  315.2 36.4 %collective-permute-done = bf16[1,128,512]{2,1,0:T(8,128)(2,1)S(1)} collective-permute-done((bf16[1,128,512]{2,1,0:T(8,128)(2,1)S(1)}, bf16[1,128,512]{2,1,0:T(8,128)(2,1)S(1)}, u32[]{:S(2)}, u32[]{:S(2)}) %collective-permute-start) | collective-permute-done | bytes 131104 | tf_op jit(solution)/shard_map/ppermute | solution.py:68
  351.6 0.2 copy.96
  351.8 0.0 collective-permute-done.1
  351.8 0.2 copy.98
  352.0 0.9 pad_maximum_fusion.4
  353.0 1.9 collective-permute-start.2
  354.9 8.7 %collective-permute-start.3 = (bf16[66,1,512]{2,0,1:T(8,128)(2,1)S(1)}, bf16[66,1,512]{2,0,1:T(8,128)(2,1)S(1)}, u32[]{:S(2)}, u32[]{:S(2)}) collective-permute-start(bf16[66,1,512]{2,0,1:T(8,128)(2,1)S(1)} %get-tuple-element.8), channel_id=1, source_target_pairs={{1,0},{2,1},{3,2},{5,4},{6,5},{7,6},{9,8},{10,9},{11,10},{13,12},{... | collective-permute-start | bytes 202760 | tf_op jit(solution)/shard_map/ppermute | solution.py:70
  363.6 82.0 %collective-permute-done.2 = bf16[66,1,512]{2,0,1:T(8,128)(2,1)S(1)} collective-permute-done((bf16[66,1,512]{2,0,1:T(8,128)(2,1)S(1)}, bf16[66,1,512]{2,0,1:T(8,128)(2,1)S(1)}, u32[]{:S(2)}, u32[]{:S(2)}) %collective-permute-start.2) | collective-permute-done | bytes 67616 | tf_op jit(solution)/shard_map/ppermute | solution.py:68
  445.6 2.0 collective-permute-done.3
  447.6 11.5 %fusion.72 = bf16[66,1,130,512]{3,0,2,1:T(8,128)(2,1)} fusion(bf16[66,1,512]{2,0,1:T(8,128)(2,1)S(1)} %collective-permute-done.3, bf16[1,128,512]{2,0,1:T(2,128)(2,1)S(1)} %copy.98, bf16[64,128,512]{2,0,1:T(8,128)(2,1)} %copy.97, bf16[1,128,512]{2,0,1:T(2,128)(2,1)S(1)} %copy.96, bf16[66,1,512]{2,0,1:T(8,128)(2,1)S(1)} %collective-permute-done.2), kind=kLoop, calls=%fused_computation.76 | loop fusion | flops 43929600 | bytes 17571840 | tf_op jit(solution)/shard_map/broadcast_in_dim | solution.py:79
  459.0 0.0 all-to-all-done.3
  459.0 4.4 copy.112
  463.4 6.0 convert_bitcast_fusion.1
  469.4 9.1 %copy.114 = bf16[512,16,384]{2,1,0:T(8,128)(2,1)} copy(bf16[512,16,384]{0,2,1:T(8,128)(2,1)} %convert_bitcast_fusion.1) | data formatting | bytes 12582912 | tf_op jit(solution)/shard_map/convert_element_type | solution.py:153
  478.5 8.6 %all-to-all-start.4 = ((bf16[512,16,384]{2,1,0:T(8,128)(2,1)}), bf16[512,16,384]{2,1,0:T(8,128)(2,1)}, u32[]{:S(2)}, u32[]{:S(2)}) async-start(bf16[512,16,384]{2,1,0:T(8,128)(2,1)} %copy.114), calls=%async_computation.4 | async-start | bytes 12582912 | tf_op jit(solution)/shard_map/all_to_all | solution.py:154
  487.1 11.5 %pad_maximum_fusion = bf16[66,130,512]{2,0,1:T(8,128)(2,1)} fusion(bf16[66,1,512]{2,0,1:T(8,128)(2,1)S(1)} %collective-permute-done.3, bf16[1,128,512]{2,0,1:T(2,128)(2,1)S(1)} %copy.98, bf16[64,128,512]{2,0,1:T(8,128)(2,1)} %copy.97, bf16[1,128,512]{2,0,1:T(2,128)(2,1)S(1)} %copy.96, bf16[66,1,512]{2,0,1:T(8,128)(2,1)S(1)} %collective-permute-done.2), kind=kLoop, calls=%fused_computation.21 | loop fusion | flops 43929600 | bytes 17571840 | tf_op jit(solution)/shard_map/concatenate | solution.py:66
  498.6 8.2 %pad = bf16[66,1,136,512]{3,0,2,1:T(8,128)(2,1)} pad(bf16[66,1,130,512]{3,0,2,1:T(8,128)(2,1)} %fusion.72, bf16[]{:T(256)} %constant.62), padding=0_0x0_0x0_6x0_0 | pad | bytes 17977346 | tf_op jit(solution)/shard_map/broadcast_in_dim | solution.py:79
  506.7 10.6 %copy.100 = bf16[66,1,8,17,512]{4,2,3,0,1:T(8,128)(2,1)} copy(bf16[66,1,8,17,512]{4,0,3,2,1:T(8,128)(2,1)} %bitcast.56) | data formatting | bytes 18382848 | tf_op jit(solution)/shard_map/conv_general_dilated | solution.py:78
  517.3 2.2 slice_bitcast_fusion.1
  519.6 0.0 copy-start.8
  519.6 0.0 copy-start.13
  519.6 0.4 pad.2
  520.0 0.3 copy.103
  520.4 0.1 slice.79
  520.4 1.3 copy-done.2
  521.7 0.3 slice.76
  522.0 0.2 copy-done.8
  522.2 21.4 %select_convert_fusion = bf16[64,8,17,128]{3,1,2,0:T(8,128)(2,1)S(1)} fusion(pred[8,17]{0,1:T(8,128)(4,1)S(1)} %copy-done.13, bf16[3,3,512,128]{3,2,1,0:T(8,128)(2,1)S(1)} %copy-done.8, bf16[66,1,7,2,512]{4,2,3,0,1:T(8,128)(2,1)S(1)} %slice.76, bf16[66,1,8,17,512]{4,2,3,0,1:T(8,128)(2,1)S(1)} %copy-done.2), kind=kOutput, calls=%fused_computation.44 | convolution fusion | flops 10300702720 | bytes 13545608 | tf_op jit(solution)/shard_map/conv_general_dilated | solution.py:78
  543.6 0.6 copy.101
  544.2 15.8 %convolution_select_fusion = f32[64,8,17,384]{3,1,2,0:T(8,128)} fusion(bf16[3,3,128,384]{3,2,1,0:T(8,128)(2,1)} %param.21, pred[8,17]{0,1:T(8,128)(4,1)S(1)} %copy-done.13, bf16[66,1,7,2,128]{4,2,3,0,1:T(8,128)(2,1)S(1)} %slice.79, bf16[66,1,8,17,128]{4,2,3,0,1:T(8,128)(2,1)S(1)} %copy.103), kind=kOutput, calls=%fused_computation.22 | convolution fusion | flops 7711789056 | bytes 16788616 | tf_op jit(solution)/shard_map/conv_general_dilated | solution.py:78
  560.0 12.2 %copy.104 = f32[64,8,17,384]{3,0,2,1:T(8,128)} copy(f32[64,8,17,384]{3,1,2,0:T(8,128)} %convolution_select_fusion) | data formatting | bytes 26738688 | tf_op jit(solution)/shard_map/conv_general_dilated | solution.py:78
  572.2 1.5 slice_bitcast_fusion.2
  573.7 8.4 %convert_bitcast_fusion = f32[64,8,16,384]{3,2,0,1:T(8,128)} fusion(bf16[8,64,16,384]{3,2,1,0:T(8,128)(2,1)} %bitcast.26), kind=kLoop, calls=%fused_computation.12 | loop fusion | flops 3145728 | bytes 18874368 | tf_op jit(solution)/shard_map/convert_element_type | solution.py:164
  582.1 12.8 %copy.115 = f32[64,8,16,384]{3,0,2,1:T(8,128)} copy(f32[64,8,16,384]{3,2,0,1:T(8,128)} %convert_bitcast_fusion) | data formatting | bytes 25165824 | tf_op jit(solution)/shard_map/convert_element_type | solution.py:164
  594.9 12.6 %fusion.8 = bf16[64,128,384]{2,0,1:T(8,128)(2,1)} fusion(f32[64,1,136,384]{3,0,2,1:T(8,128)} %bitcast.55, f32[64,8,16,384]{3,0,2,1:T(8,128)} %copy.115), kind=kLoop, calls=%fused_computation.11 | loop fusion | flops 6291456 | bytes 31457280 | tf_op jit(solution)/shard_map/convert_element_type | solution.py:164
  607.5 0.0 copy-start.1
  607.5 7.8 %pad_maximum_fusion.1 = bf16[64,128,512]{2,0,1:T(8,128)(2,1)} fusion(bf16[64,128,384]{2,0,1:T(8,128)(2,1)} %fusion.8, bf16[64,128,128]{2,0,1:T(8,128)(2,1)S(1)} %copy-done.3), kind=kLoop, calls=%fused_computation.27 | loop fusion | flops 16777216 | bytes 16777216 | tf_op jit(solution)/shard_map/concatenate | solution.py:163
  615.3 11.5 %copy.116 = bf16[64,128,512]{2,1,0:T(8,128)(2,1)} copy(bf16[64,128,512]{2,0,1:T(8,128)(2,1)} %pad_maximum_fusion.1) | data formatting | bytes 16777216 | tf_op jit(solution)/shard_map/concatenate | solution.py:163
  (28 shorter events, 0.1 us)
Async XLA Ops:
  0.0 261.0 %copy-start = (bf16[768,768]{1,0:T(8,128)(2,1)S(1)}, bf16[768,768]{1,0:T(8,128)(2,1)}, u32[]{:S(2)}) copy-start(bf16[768,768]{1,0:T(8,128)(2,1)} %param.22) | copy-start | bytes 3538948
  11.6 2.8 slice-start
  88.8 3.8 copy-start.12
  103.2 5.9 copy-start.6
  103.2 5.9 copy-start.7
  103.2 6.0 copy-start.4
  103.2 6.0 copy-start.5
  103.2 143.4 %all-to-all-start.1 = ((bf16[512,16,384]{2,1,0:T(8,128)(2,1)}), bf16[512,16,384]{2,1,0:T(8,128)(2,1)}, u32[]{:S(2)}, u32[]{:S(2)}) async-start(bf16[512,16,384]{2,1,0:T(8,128)(2,1)} %copy.108), calls=%async_computation.1 | async-start | bytes 12582912 | tf_op jit(solution)/shard_map/all_to_all | solution.py:133
  109.1 141.4 %copy-start.9 = (bf16[1056,1024]{1,0:T(8,128)(2,1)S(1)}, bf16[1056,1024]{1,0:T(8,128)(2,1)}, u32[]{:S(2)}) copy-start(bf16[1056,1024]{1,0:T(8,128)(2,1)} %constant.91) | copy-start | bytes 6488068
  246.6 3.9 copy-start.10
  268.8 13.1 %all-to-all-start.2 = ((f32[32,1,768]{2,1,0:T(1,128)}), f32[32,1,768]{2,1,0:T(1,128)S(1)}, u32[]{:S(2)}, u32[]{:S(2)}) async-start(f32[32,1,768]{2,1,0:T(1,128)} %broadcast_in_dim.112), calls=%async_computation.2 | async-start | bytes 196608 | tf_op jit(solution)/shard_map/all_to_all | solution.py:139
  303.0 156.1 %all-to-all-start.3 = ((bf16[16,512,384]{2,0,1:T(8,128)(2,1)}), bf16[16,512,384]{2,0,1:T(8,128)(2,1)}, u32[]{:S(2)}, u32[]{:S(2)}) async-start(bf16[16,512,384]{2,0,1:T(8,128)(2,1)} %copy.111), calls=%async_computation.3 | async-start | bytes 12582912 | tf_op jit(solution)/shard_map/all_to_all | solution.py:152
  309.9 41.7 %collective-permute-start = (bf16[1,128,512]{2,1,0:T(8,128)(2,1)S(1)}, bf16[1,128,512]{2,1,0:T(8,128)(2,1)S(1)}, u32[]{:S(2)}, u32[]{:S(2)}) collective-permute-start(bf16[1,128,512]{2,1,0:T(8,128)(2,1)S(1)} %get-tuple-element.9), channel_id=1, source_target_pairs={{0,4},{4,8},{8,12},{12,16},{16,20},{20,24},{24,28},{1,5},{5,9},{9,... | collective-permute-start | bytes 393224 | tf_op jit(solution)/shard_map/ppermute | solution.py:68
  313.2 38.6 %collective-permute-start.1 = (bf16[1,128,512]{2,1,0:T(8,128)(2,1)S(1)}, bf16[1,128,512]{2,1,0:T(8,128)(2,1)S(1)}, u32[]{:S(2)}, u32[]{:S(2)}) collective-permute-start(bf16[1,128,512]{2,1,0:T(8,128)(2,1)S(1)} %get-tuple-element.10), channel_id=1, source_target_pairs={{4,0},{8,4},{12,8},{16,12},{20,16},{24,20},{28,24},{5,1},{9,5},{13... | collective-permute-start | bytes 393224 | tf_op jit(solution)/shard_map/ppermute | solution.py:70
  353.0 92.6 %collective-permute-start.2 = (bf16[66,1,512]{2,0,1:T(8,128)(2,1)S(1)}, bf16[66,1,512]{2,0,1:T(8,128)(2,1)S(1)}, u32[]{:S(2)}, u32[]{:S(2)}) collective-permute-start(bf16[66,1,512]{2,0,1:T(8,128)(2,1)S(1)} %get-tuple-element.7), channel_id=1, source_target_pairs={{0,1},{1,2},{2,3},{4,5},{5,6},{6,7},{8,9},{9,10},{10,11},{12,13},{... | collective-permute-start | bytes 202760 | tf_op jit(solution)/shard_map/ppermute | solution.py:68
  354.9 92.7 %collective-permute-start.3 = (bf16[66,1,512]{2,0,1:T(8,128)(2,1)S(1)}, bf16[66,1,512]{2,0,1:T(8,128)(2,1)S(1)}, u32[]{:S(2)}, u32[]{:S(2)}) collective-permute-start(bf16[66,1,512]{2,0,1:T(8,128)(2,1)S(1)} %get-tuple-element.8), channel_id=1, source_target_pairs={{1,0},{2,1},{3,2},{5,4},{6,5},{7,6},{9,8},{10,9},{11,10},{13,12},{... | collective-permute-start | bytes 202760 | tf_op jit(solution)/shard_map/ppermute | solution.py:70
  459.0 4.4 copy-start.11
  478.5 95.2 %all-to-all-start.4 = ((bf16[512,16,384]{2,1,0:T(8,128)(2,1)}), bf16[512,16,384]{2,1,0:T(8,128)(2,1)}, u32[]{:S(2)}, u32[]{:S(2)}) async-start(bf16[512,16,384]{2,1,0:T(8,128)(2,1)} %copy.114), calls=%async_computation.4 | async-start | bytes 12582912 | tf_op jit(solution)/shard_map/all_to_all | solution.py:154
  517.3 4.3 copy-start.2
  519.6 2.6 copy-start.8
  519.6 2.6 copy-start.13
  594.9 12.6 %copy-start.3 = (bf16[64,128,128]{2,0,1:T(8,128)(2,1)S(1)}, bf16[64,128,128]{2,0,1:T(8,128)(2,1)}, u32[]{:S(2)}) copy-start(bf16[64,128,128]{2,0,1:T(8,128)(2,1)} %slice_bitcast_fusion.2) | copy-start | bytes 6291460
  607.5 19.3 %copy-start.1 = (bf16[768,768]{1,0:T(8,128)(2,1)S(1)}, bf16[768,768]{1,0:T(8,128)(2,1)}, u32[]{:S(2)}) copy-start(bf16[768,768]{1,0:T(8,128)(2,1)} %param.22) | copy-start | bytes 3538948
where the time goes:
time: 632 us; the launch traced here: 627 us
  waiting for transfers between devices  258 us (41%)
  local copies, waits for them, and re-layouts  120 us (19%)
  matrix products  78.9 us (12%)
  blocking collectives  74.4 us (12%)
  other arithmetic  52.8 us (8%)
  starting transfers between devices  43.1 us (7%)
    all_to_all x1, waiting for transfers between devices, global_branch(): lines = lax.all_to_all(field, BOTH, split_axis=0, concat_axis=1, tiled=True)  137 us
    ppermute x2, waiting for transfers between devices, extended(): lax.ppermute(tail, axis, [(i, (i + 1) % count) for i in range(ends)])  118 us
    all_to_all x1, blocking collectives, global_branch(): lax.all_to_all(glob, 'row', split_axis=1, concat_axis=0, tiled=True)  74.4 us
    dot_general x5, matrix products, product(): return jnp.einsum(form, left, right, preferred_element_type=jnp.float32)  41.7 us
    conv_general_dilated x2, matrix products, conv(): lax.conv_general_dilated(padded[None], weight, (1, 1), 'VALID', dimension...  37.2 us
    conv_general_dilated x5, local copies, waits for them, and re-layouts, conv(): lax.conv_general_dilated(padded[None], weight, (1, 1), 'VALID', dimension...  23.4 us
    unnamed x29, local copies, waits for them, and re-layouts  13.2 us
    convert_element_type x1, local copies, waits for them, and re-layouts, body(): cross_out + spectral  12.8 us
  transfers between devices with their start and end apart: 8, of which 4 were waited for; matrix products, arithmetic and copies ran while one was open for 17% of the time, Pallas kernels for 0%

commit v1 on v0

--- a/solution.py
+++ b/solution.py
@@ -95,7 +95,19 @@
     height, width, ch = (glob.shape[0] * nrow, glob.shape[1] * ncol, glob.shape[2])
     bins = height // (2 * count)
     padded = -(-(width + 2) // 16) * 16
-    columns = lax.all_to_all(glob, "row", split_axis=1, concat_axis=0, tiled=True)
+    ways, here = (lax.axis_size("row"), lax.axis_index("row"))
+    width_2 = glob.shape[1] // ways
+    shape = list(glob.shape)
+    shape[1] = width_2
+    height_2 = shape[0]
+    shape[0] = height_2 * ways
+    full = jnp.zeros(shape, glob.dtype)
+    for mask in range(ways):
+        part_2 = lax.dynamic_slice_in_dim(glob, (here ^ mask) * width_2, width_2, axis=1)
+        if mask:
+            part_2 = lax.ppermute(part_2, "row", [(d, d ^ mask) for d in range(ways)])
+        full = lax.dynamic_update_slice_in_dim(full, part_2, (here ^ mask) * height_2, axis=0)
+    columns = full
     col_np = column_table(height)
     plain_np, packed_np, sign, upper, lower, scale_plain, scale_packed = width_tables(
         width_order(nrow, ncol, width), width, padded

time: 632 us -> 700 us (1.11); the launches traced: 627 us -> 687 us
  local copies, waits for them, and re-layouts: 120 us -> 240 us
  blocking collectives: 74.4 us -> 0 us
  starting transfers between devices: 43.1 us -> 53 us
    dynamic_update_slice x0 -> x8, local copies, waits for them, and re-layouts: none -> 95.9 us  [global_branch(): lax.dynamic_update_slice_in_dim(full, part_2, (here ^ mask) * height_2, a...]
    all_to_all x1 -> x0, blocking collectives: 74.4 us -> none  [global_branch(): lax.all_to_all(glob, 'row', split_axis=1, concat_axis=0, tiled=True)]
    ppermute x0 -> x7, waiting for transfers between devices: none -> 14.1 us  [global_branch(): part_2 = lax.ppermute(part_2, 'row', [(d, d ^ mask) for d in range(ways)])]
    ppermute x0 -> x7, local copies, waits for them, and re-layouts: none -> 11.9 us  [global_branch(): part_2 = lax.ppermute(part_2, 'row', [(d, d ^ mask) for d in range(ways)])]
    ppermute x2, waiting for transfers between devices: 118 us -> 107 us  [extended(): lax.ppermute(tail, axis, [(i, (i + 1) % count) for i in range(ends)])]
    ppermute x0 -> x7, starting transfers between devices: none -> 9.53 us  [global_branch(): part_2 = lax.ppermute(part_2, 'row', [(d, d ^ mask) for d in range(ways)])]
  transfers between devices with their start and end apart: 8 -> 15, of which waited for: 4 -> 5; matrix products, arithmetic and copies ran while one was open for 17% -> 31% of each run, Pallas kernels for 0% -> 0%
where the time goes in v1:
time: 700 us; the launch traced here: 687 us
  waiting for transfers between devices  260 us (37%)
  local copies, waits for them, and re-layouts  240 us (34%)
  matrix products  82.6 us (12%)
  starting transfers between devices  53 us (8%)
  other arithmetic  50.1 us (7%)
    all_to_all x1, waiting for transfers between devices, global_branch(): lines = lax.all_to_all(field, BOTH, split_axis=0, concat_axis=1, tiled=True)  137 us
    ppermute x2, waiting for transfers between devices, extended(): lax.ppermute(tail, axis, [(i, (i + 1) % count) for i in range(ends)])  107 us
    dynamic_update_slice x8, local copies, waits for them, and re-layouts, global_branch(): lax.dynamic_update_slice_in_dim(full, part_2, (here ^ mask) * height_2, a...  95.9 us
    dot_general x5, matrix products, product(): return jnp.einsum(form, left, right, preferred_element_type=jnp.float32)  45.7 us
    conv_general_dilated x2, matrix products, conv(): lax.conv_general_dilated(padded[None], weight, (1, 1), 'VALID', dimension...  36.9 us
    conv_general_dilated x5, local copies, waits for them, and re-layouts, conv(): lax.conv_general_dilated(padded[None], weight, (1, 1), 'VALID', dimension...  23.5 us
    ppermute x7, waiting for transfers between devices, global_branch(): part_2 = lax.ppermute(part_2, 'row', [(d, d ^ mask) for d in range(ways)])  14.1 us
  transfers between devices with their start and end apart: 15, of which 5 were waited for; matrix products, arithmetic and copies ran while one was open for 31% of the time, Pallas kernels for 0%

profile of v1, /device:TPU:11, one launch (start us, length us, event | category | flops | bytes accessed | tf_op | source)
XLA Modules:
  0.0 687.2 jit_solution(1228403910503429463)
XLA Ops:
  0.0 6.8 slice.63
  6.8 4.9 constant_dynamic-slice_fusion
  11.9 1.0 collective-permute-start.4
  12.8 1.1 collective-permute-start.6
  13.9 1.2 collective-permute-start.7
  16.1 14.1 %collective-permute-done.5 = bf16[64,16,384]{2,1,0:T(8,128)(2,1)S(1)} collective-permute-done((bf16[64,16,384]{2,1,0:T(8,128)(2,1)S(1)}, bf16[64,16,384]{2,1,0:T(8,128)(2,1)S(1)}, u32[]{:S(2)}, u32[]{:S(2)}) %collective-permute-start.5) | collective-permute-done | bytes 786464 | tf_op jit(solution)/shard_map/ppermute | solution.py:108
  30.2 1.2 collective-permute-start.9
  32.2 3.9 collective-permute-start.10
  37.1 3.3 broadcast_in_dim.109
  40.4 13.5 %dynamic_update_slice.24 = bf16[512,16,384]{0,2,1:T(8,128)(2,1)} dynamic-update-slice(bf16[512,16,384]{0,2,1:T(8,128)(2,1)} %broadcast_in_dim.109, bf16[64,16,384]{0,2,1:T(8,128)(2,1)S(1)} %copy.136, s32[]{:T(128)S(6)} %select_n.67, s32[]{:T(128)} %constant.20.clone.1, s32[]{:T(128)} %constant.20.clone.1) | dynamic-update-slice | bytes 1572868 | tf_op jit(solution)/shard_map/dynamic_update_slice | solution.py:109
  53.9 1.8 copy.137
  55.7 10.8 %dynamic_update_slice.25 = bf16[512,16,384]{0,2,1:T(8,128)(2,1)} dynamic-update-slice(bf16[512,16,384]{0,2,1:T(8,128)(2,1)} %dynamic_update_slice.24, bf16[64,16,384]{0,2,1:T(8,128)(2,1)S(1)} %copy.137, s32[]{:T(128)S(6)} %select_n.69, s32[]{:T(128)} %constant.20.clone.1, s32[]{:T(128)} %constant.20.clone.1) | dynamic-update-slice | bytes 1572868 | tf_op jit(solution)/shard_map/dynamic_update_slice | solution.py:109
  66.5 0.9 copy.138
  67.5 13.5 %dynamic_update_slice.26 = bf16[512,16,384]{0,2,1:T(8,128)(2,1)} dynamic-update-slice(bf16[512,16,384]{0,2,1:T(8,128)(2,1)} %dynamic_update_slice.25, bf16[64,16,384]{0,2,1:T(8,128)(2,1)S(1)} %copy.138, s32[]{:T(128)S(6)} %select_n.71, s32[]{:T(128)} %constant.20.clone.1, s32[]{:T(128)} %constant.20.clone.1) | dynamic-update-slice | bytes 1572868 | tf_op jit(solution)/shard_map/dynamic_update_slice | solution.py:109
  81.0 1.8 copy.139
  82.8 10.8 %dynamic_update_slice.27 = bf16[512,16,384]{0,2,1:T(8,128)(2,1)} dynamic-update-slice(bf16[512,16,384]{0,2,1:T(8,128)(2,1)} %dynamic_update_slice.26, bf16[64,16,384]{0,2,1:T(8,128)(2,1)S(1)} %copy.139, s32[]{:T(128)S(6)} %select_n.73, s32[]{:T(128)} %constant.20.clone.1, s32[]{:T(128)} %constant.20.clone.1) | dynamic-update-slice | bytes 1572868 | tf_op jit(solution)/shard_map/dynamic_update_slice | solution.py:109
  93.6 1.8 copy.140
  95.5 12.8 %dynamic_update_slice.28 = bf16[512,16,384]{0,2,1:T(8,128)(2,1)} dynamic-update-slice(bf16[512,16,384]{0,2,1:T(8,128)(2,1)} %dynamic_update_slice.27, bf16[64,16,384]{0,2,1:T(8,128)(2,1)S(1)} %copy.140, s32[]{:T(128)S(6)} %select_n.75, s32[]{:T(128)} %constant.20.clone.1, s32[]{:T(128)} %constant.20.clone.1) | dynamic-update-slice | bytes 1572868 | tf_op jit(solution)/shard_map/dynamic_update_slice | solution.py:109
  108.3 1.8 copy.141
  110.1 10.1 %dynamic_update_slice.29 = bf16[512,16,384]{0,2,1:T(8,128)(2,1)} dynamic-update-slice(bf16[512,16,384]{0,2,1:T(8,128)(2,1)} %dynamic_update_slice.28, bf16[64,16,384]{0,2,1:T(8,128)(2,1)S(1)} %copy.141, s32[]{:T(128)S(6)} %select_n.77, s32[]{:T(128)} %constant.20.clone.1, s32[]{:T(128)} %constant.20.clone.1) | dynamic-update-slice | bytes 1572868 | tf_op jit(solution)/shard_map/dynamic_update_slice | solution.py:109
  120.2 1.8 copy.142
  122.1 13.5 %dynamic_update_slice.30 = bf16[512,16,384]{0,2,1:T(8,128)(2,1)} dynamic-update-slice(bf16[512,16,384]{0,2,1:T(8,128)(2,1)} %dynamic_update_slice.29, bf16[64,16,384]{0,2,1:T(8,128)(2,1)S(1)} %copy.142, s32[]{:T(128)S(6)} %select_n.79, s32[]{:T(128)} %constant.20.clone.1, s32[]{:T(128)} %constant.20.clone.1) | dynamic-update-slice | bytes 1572868 | tf_op jit(solution)/shard_map/dynamic_update_slice | solution.py:109
  135.6 1.8 copy.143
  137.4 10.8 %dynamic_update_slice.31 = bf16[512,16,384]{0,2,1:T(8,128)(2,1)} dynamic-update-slice(bf16[512,16,384]{0,2,1:T(8,128)(2,1)} %dynamic_update_slice.30, bf16[64,16,384]{0,2,1:T(8,128)(2,1)S(1)} %copy.143, s32[]{:T(128)S(6)} %select_n.81, s32[]{:T(128)} %constant.20.clone.1, s32[]{:T(128)} %constant.20.clone.1) | dynamic-update-slice | bytes 1572868 | tf_op jit(solution)/shard_map/dynamic_update_slice | solution.py:109
  148.2 8.1 %convert_bitcast_fusion.2 = bf16[512,16,384]{0,2,1:T(8,128)(2,1)} fusion(bf16[512,16,384]{0,2,1:T(8,128)(2,1)} %dynamic_update_slice.31, bf16[512,512,1]{1,0,2:T(8,128)(2,1)S(1)} %copy-done.16), kind=kOutput, calls=%fused_computation.39 | convolution fusion | flops 3224371200 | bytes 13107200 | tf_op jit(solution)/shard_map/uh,hwc->uwc/dot_general | solution.py:89
  156.4 9.1 %copy.144 = bf16[512,16,384]{2,1,0:T(8,128)(2,1)} copy(bf16[512,16,384]{0,2,1:T(8,128)(2,1)} %convert_bitcast_fusion.2) | data formatting | bytes 12582912 | tf_op jit(solution)/shard_map/convert_element_type | solution.py:144
  165.5 6.5 all-to-all-start
  172.2 137.3 %all-to-all-done = bf16[512,16,384]{2,1,0:T(8,128)(2,1)} async-done(((bf16[512,16,384]{2,1,0:T(8,128)(2,1)}), bf16[512,16,384]{2,1,0:T(8,128)(2,1)}, u32[]{:S(2)}, u32[]{:S(2)}) %all-to-all-start) | async-done | bytes 6291488 | tf_op jit(solution)/shard_map/all_to_all | solution.py:145
  309.4 3.9 copy.145
  313.4 9.8 %fusion.20 = bf16[8,1056,384]{2,1,0:T(8,128)(2,1)S(1)} fusion(bf16[8,1024,384]{2,1,0:T(8,128)(2,1)S(1)} %bitcast.63, pred[8]{0:T(512)(128)(4,1)S(1)} %compare_and_fusion, bf16[1056,1024]{1,0:T(8,128)(2,1)S(1)} %copy-done.13, bf16[1056,1024]{1,0:T(8,128)(2,1)S(1)} %copy-done.14), kind=kOutput, calls=%fused_computation.28 | convolution fusion | flops 6655672320 | bytes 17104904 | tf_op jit(solution)/shard_map/bmk,bkc->bmc/dot_general | solution.py:89
  323.8 7.2 %maximum_reduce_fusion = (f32[768]{0:T(1024)S(1)}, bf16[8,528,768]{2,1,0:T(8,128)(2,1)}) fusion(f32[8,528]{1,0:T(8,128)S(1)} %broadcast_select_fusion.1, bf16[768,768]{1,0:T(8,128)(2,1)S(1)} %copy-done, bf16[8,528,384]{2,1,0:T(8,128)(2,1)S(1)} %get-tuple-element.14, bf16[8,528,384]{2,1,0:T(8,128)(2,1)S(1)} %get-tuple-element.13), kind=kOutput, calls=%fused_computation.14 | convolution fusion | flops 5008784384 | bytes 14175744 | tf_op jit(solution)/shard_map/bvc,co->bvo/dot_general | solution.py:89
  331.6 6.4 all-to-all-start.1
  338.0 6.3 fusion.59
  344.4 14.6 %subtract_convert_fusion = bf16[8,1024,384]{2,1,0:T(8,128)(2,1)S(1)} fusion(bf16[8,528,384]{2,1,0:T(8,128)(2,1)} %get-tuple-element.12, bf16[8,528,384]{2,1,0:T(8,128)(2,1)} %get-tuple-element.11, pred[8]{0:T(512)(128)(4,1)S(1)} %compare_and_fusion, bf16[1056,1024]{1,0:T(8,128)(2,1)S(1)} %copy-done.13, bf16[1056,1024]{1,0:T(8,128)(2,1)} %constant.104, ...), kind=kOutput, calls=%fused_computation.13 | convolution fusion | flops 6681133056 | bytes 17173512 | tf_op jit(solution)/shard_map/bkm,bkc->bmc/dot_general | solution.py:89
  359.0 6.4 copy.147
  365.4 5.9 all-to-all-start.2
  371.3 1.0 fusion.58
  372.3 3.4 collective-permute-start
  375.7 2.1 collective-permute-start.1
  377.9 11.5 %copy.128 = bf16[64,128,512]{2,0,1:T(8,128)(2,1)} copy(bf16[64,128,512]{2,1,0:T(8,128)(2,1)} %param.19) | data formatting | bytes 16777216 | tf_op args[0]
  389.4 24.7 %collective-permute-done = bf16[1,128,512]{2,1,0:T(8,128)(2,1)S(1)} collective-permute-done((bf16[1,128,512]{2,1,0:T(8,128)(2,1)S(1)}, bf16[1,128,512]{2,1,0:T(8,128)(2,1)S(1)}, u32[]{:S(2)}, u32[]{:S(2)}) %collective-permute-start) | collective-permute-done | bytes 131104 | tf_op jit(solution)/shard_map/ppermute | solution.py:68
  415.4 1.9 collective-permute-start.2
  417.4 8.5 %collective-permute-start.3 = (bf16[66,1,512]{2,0,1:T(8,128)(2,1)S(1)}, bf16[66,1,512]{2,0,1:T(8,128)(2,1)S(1)}, u32[]{:S(2)}, u32[]{:S(2)}) collective-permute-start(bf16[66,1,512]{2,0,1:T(8,128)(2,1)S(1)} %get-tuple-element.8), channel_id=1, source_target_pairs={{1,0},{2,1},{3,2},{5,4},{6,5},{7,6},{9,8},{10,9},{11,10},{13,12},{... | collective-permute-start | bytes 202760 | tf_op jit(solution)/shard_map/ppermute | solution.py:70
  425.9 82.1 %collective-permute-done.2 = bf16[66,1,512]{2,0,1:T(8,128)(2,1)S(1)} collective-permute-done((bf16[66,1,512]{2,0,1:T(8,128)(2,1)S(1)}, bf16[66,1,512]{2,0,1:T(8,128)(2,1)S(1)}, u32[]{:S(2)}, u32[]{:S(2)}) %collective-permute-start.2) | collective-permute-done | bytes 67616 | tf_op jit(solution)/shard_map/ppermute | solution.py:68
  508.0 2.0 collective-permute-done.3
  510.0 8.7 %fusion.68 = bf16[66,1,130,512]{3,0,2,1:T(8,128)(2,1)} fusion(bf16[66,1,512]{2,0,1:T(8,128)(2,1)S(1)} %collective-permute-done.3, bf16[1,128,512]{2,0,1:T(2,128)(2,1)S(1)} %copy.129, bf16[64,128,512]{2,0,1:T(8,128)(2,1)S(1)} %copy-done.2, bf16[1,128,512]{2,0,1:T(2,128)(2,1)S(1)} %copy.127, bf16[66,1,512]{2,0,1:T(8,128)(2,1)S(1)} %collective-permute-done.2), kind=kLoop, calls=%fused_computation.82 | loop fusion | flops 43929600 | bytes 17571840 | tf_op jit(solution)/shard_map/broadcast_in_dim | solution.py:79
  518.7 4.4 copy.148
  523.1 6.0 convert_bitcast_fusion.1
  529.1 9.1 %copy.150 = bf16[512,16,384]{2,1,0:T(8,128)(2,1)} copy(bf16[512,16,384]{0,2,1:T(8,128)(2,1)} %convert_bitcast_fusion.1) | data formatting | bytes 12582912 | tf_op jit(solution)/shard_map/convert_element_type | solution.py:165
  538.2 8.8 %all-to-all-start.3 = ((bf16[512,16,384]{2,1,0:T(8,128)(2,1)}), bf16[512,16,384]{2,1,0:T(8,128)(2,1)}, u32[]{:S(2)}, u32[]{:S(2)}) async-start(bf16[512,16,384]{2,1,0:T(8,128)(2,1)} %copy.150), calls=%async_computation.3 | async-start | bytes 12582912 | tf_op jit(solution)/shard_map/all_to_all | solution.py:166
  547.0 11.5 %pad_maximum_fusion = bf16[66,130,512]{2,0,1:T(8,128)(2,1)} fusion(bf16[66,1,512]{2,0,1:T(8,128)(2,1)S(1)} %collective-permute-done.3, bf16[1,128,512]{2,0,1:T(2,128)(2,1)S(1)} %copy.129, bf16[64,128,512]{2,0,1:T(8,128)(2,1)} %copy.128, bf16[1,128,512]{2,0,1:T(2,128)(2,1)S(1)} %copy.127, bf16[66,1,512]{2,0,1:T(8,128)(2,1)S(1)} %collective-permute-done.2), kind=kLoop, calls=%fused_computation.21 | loop fusion | flops 43929600 | bytes 17571840 | tf_op jit(solution)/shard_map/concatenate | solution.py:66
  558.5 8.2 %pad = bf16[66,1,136,512]{3,0,2,1:T(8,128)(2,1)} pad(bf16[66,1,130,512]{3,0,2,1:T(8,128)(2,1)} %fusion.68, bf16[]{:T(256)} %constant.21.clone.1), padding=0_0x0_0x0_6x0_0 | pad | bytes 17977346 | tf_op jit(solution)/shard_map/broadcast_in_dim | solution.py:79
  566.7 10.6 %copy.131 = bf16[66,1,8,17,512]{4,2,3,0,1:T(8,128)(2,1)} copy(bf16[66,1,8,17,512]{4,0,3,2,1:T(8,128)(2,1)} %bitcast.58) | data formatting | bytes 18382848 | tf_op jit(solution)/shard_map/conv_general_dilated | solution.py:78
  577.3 2.2 slice_bitcast_fusion.1
  580.4 1.3 copy-done.3
  582.2 21.4 %select_convert_fusion = bf16[64,8,17,128]{3,1,2,0:T(8,128)(2,1)S(1)} fusion(pred[8,17]{0,1:T(8,128)(4,1)S(1)} %copy-done.17, bf16[3,3,512,128]{3,2,1,0:T(8,128)(2,1)S(1)} %copy-done.12, bf16[66,1,7,2,512]{4,2,3,0,1:T(8,128)(2,1)S(1)} %slice.76, bf16[66,1,8,17,512]{4,2,3,0,1:T(8,128)(2,1)S(1)} %copy-done.3), kind=kOutput, calls=%fused_computation.43 | convolution fusion | flops 10300702720 | bytes 13545608 | tf_op jit(solution)/shard_map/conv_general_dilated | solution.py:78
  604.1 15.6 %convolution_select_fusion = f32[64,8,17,384]{3,1,2,0:T(8,128)} fusion(bf16[3,3,128,384]{3,2,1,0:T(8,128)(2,1)} %param.21, pred[8,17]{0,1:T(8,128)(4,1)S(1)} %copy-done.17, bf16[66,1,7,2,128]{4,2,3,0,1:T(8,128)(2,1)S(1)} %slice.79, bf16[66,1,8,17,128]{4,2,3,0,1:T(8,128)(2,1)S(1)} %copy.134), kind=kOutput, calls=%fused_computation.22 | convolution fusion | flops 7711789056 | bytes 16788616 | tf_op jit(solution)/shard_map/conv_general_dilated | solution.py:78
  619.7 12.2 %copy.135 = f32[64,8,17,384]{3,0,2,1:T(8,128)} copy(f32[64,8,17,384]{3,1,2,0:T(8,128)} %convolution_select_fusion) | data formatting | bytes 26738688 | tf_op jit(solution)/shard_map/conv_general_dilated | solution.py:78
  631.9 1.5 slice_bitcast_fusion.2
  633.4 8.4 %convert_bitcast_fusion = f32[64,8,16,384]{3,2,0,1:T(8,128)} fusion(bf16[8,64,16,384]{3,2,1,0:T(8,128)(2,1)} %bitcast.26), kind=kLoop, calls=%fused_computation.12 | loop fusion | flops 3145728 | bytes 18874368 | tf_op jit(solution)/shard_map/convert_element_type | solution.py:176
  641.8 12.8 %copy.151 = f32[64,8,16,384]{3,0,2,1:T(8,128)} copy(f32[64,8,16,384]{3,2,0,1:T(8,128)} %convert_bitcast_fusion) | data formatting | bytes 25165824 | tf_op jit(solution)/shard_map/convert_element_type | solution.py:176
  654.7 12.7 %fusion.8 = bf16[64,128,384]{2,0,1:T(8,128)(2,1)} fusion(f32[64,1,136,384]{3,0,2,1:T(8,128)} %bitcast.57, f32[64,8,16,384]{3,0,2,1:T(8,128)} %copy.151), kind=kLoop, calls=%fused_computation.11 | loop fusion | flops 6291456 | bytes 31457280 | tf_op jit(solution)/shard_map/convert_element_type | solution.py:176
  667.4 7.8 %pad_maximum_fusion.1 = bf16[64,128,512]{2,0,1:T(8,128)(2,1)} fusion(bf16[64,128,384]{2,0,1:T(8,128)(2,1)} %fusion.8, bf16[64,128,128]{2,0,1:T(8,128)(2,1)S(1)} %copy-done.4), kind=kLoop, calls=%fused_computation.27 | loop fusion | flops 16777216 | bytes 16777216 | tf_op jit(solution)/shard_map/concatenate | solution.py:175
  675.1 11.5 %copy.152 = bf16[64,128,512]{2,1,0:T(8,128)(2,1)} copy(bf16[64,128,512]{2,0,1:T(8,128)(2,1)} %pad_maximum_fusion.1) | data formatting | bytes 16777216 | tf_op jit(solution)/shard_map/concatenate | solution.py:175
  (65 shorter events, 7.8 us)
Async XLA Ops:
  0.0 323.8 %copy-start = (bf16[768,768]{1,0:T(8,128)(2,1)S(1)}, bf16[768,768]{1,0:T(8,128)(2,1)}, u32[]{:S(2)}) copy-start(bf16[768,768]{1,0:T(8,128)(2,1)} %param.22) | copy-start | bytes 3538948
  11.6 18.5 %collective-permute-start.5 = (bf16[64,16,384]{2,1,0:T(8,128)(2,1)S(1)}, bf16[64,16,384]{2,1,0:T(8,128)(2,1)S(1)}, u32[]{:S(2)}, u32[]{:S(2)}) collective-permute-start(bf16[64,16,384]{2,1,0:T(8,128)(2,1)S(1)} %get-tuple-element.20), channel_id=1, source_target_pairs={{0,8},{4,12},{8,0},{12,4},{16,24},{20,28},{24,16},{28,20},{1,9},{5... | collective-permute-start | bytes 2359304 | tf_op jit(solution)/shard_map/ppermute | solution.py:108
  11.9 19.5 %collective-permute-start.4 = (bf16[64,16,384]{2,1,0:T(8,128)(2,1)S(1)}, bf16[64,16,384]{2,1,0:T(8,128)(2,1)S(1)}, u32[]{:S(2)}, u32[]{:S(2)}) collective-permute-start(bf16[64,16,384]{2,1,0:T(8,128)(2,1)S(1)} %get-tuple-element.21), channel_id=1, source_target_pairs={{0,4},{4,0},{8,12},{12,8},{16,20},{20,16},{24,28},{28,24},{1,5},{5... | collective-permute-start | bytes 2359304 | tf_op jit(solution)/shard_map/ppermute | solution.py:108
  12.8 68.2 %collective-permute-start.6 = (bf16[64,16,384]{2,1,0:T(8,128)(2,1)}, bf16[64,16,384]{2,1,0:T(8,128)(2,1)}, u32[]{:S(2)}, u32[]{:S(2)}) collective-permute-start(bf16[64,16,384]{2,1,0:T(8,128)(2,1)} %get-tuple-element.19), channel_id=1, source_target_pairs={{0,12},{4,8},{8,4},{12,0},{16,28},{20,24},{24,20},{28,16},{1,13},{... | collective-permute-start | bytes 2359304 | tf_op jit(solution)/shard_map/ppermute | solution.py:108
  13.9 79.7 %collective-permute-start.7 = (bf16[64,16,384]{2,1,0:T(8,128)(2,1)}, bf16[64,16,384]{2,1,0:T(8,128)(2,1)}, u32[]{:S(2)}, u32[]{:S(2)}) collective-permute-start(bf16[64,16,384]{2,1,0:T(8,128)(2,1)} %get-tuple-element.18), channel_id=1, source_target_pairs={{0,16},{4,20},{8,24},{12,28},{16,0},{20,4},{24,8},{28,12},{1,17},{... | collective-permute-start | bytes 2359304 | tf_op jit(solution)/shard_map/ppermute | solution.py:108
  15.2 93.1 %collective-permute-start.8 = (bf16[64,16,384]{2,1,0:T(8,128)(2,1)}, bf16[64,16,384]{2,1,0:T(8,128)(2,1)}, u32[]{:S(2)}, u32[]{:S(2)}) collective-permute-start(bf16[64,16,384]{2,1,0:T(8,128)(2,1)} %get-tuple-element.17), channel_id=1, source_target_pairs={{0,20},{4,16},{8,28},{12,24},{16,4},{20,0},{24,12},{28,8},{1,21},{... | collective-permute-start | bytes 2359304 | tf_op jit(solution)/shard_map/ppermute | solution.py:108
  30.1 1.2 copy-start.5
  30.2 90.1 %collective-permute-start.9 = (bf16[64,16,384]{2,1,0:T(8,128)(2,1)}, bf16[64,16,384]{2,1,0:T(8,128)(2,1)}, u32[]{:S(2)}, u32[]{:S(2)}) collective-permute-start(bf16[64,16,384]{2,1,0:T(8,128)(2,1)} %get-tuple-element.16), channel_id=1, source_target_pairs={{0,24},{4,28},{8,16},{12,20},{16,8},{20,12},{24,0},{28,4},{1,25},{... | collective-permute-start | bytes 2359304 | tf_op jit(solution)/shard_map/ppermute | solution.py:108
  31.4 0.9 copy-start.7
  32.2 103.4 %collective-permute-start.10 = (bf16[64,16,384]{2,1,0:T(8,128)(2,1)}, bf16[64,16,384]{2,1,0:T(8,128)(2,1)}, u32[]{:S(2)}, u32[]{:S(2)}) collective-permute-start(bf16[64,16,384]{2,1,0:T(8,128)(2,1)} %get-tuple-element.15), channel_id=1, source_target_pairs={{0,28},{4,24},{8,20},{12,16},{16,12},{20,8},{24,4},{28,0},{1,29},{... | collective-permute-start | bytes 2359304 | tf_op jit(solution)/shard_map/ppermute | solution.py:108
  37.1 29.5 %copy-start.6 = (bf16[64,16,384]{2,1,0:T(8,128)(2,1)S(1)}, bf16[64,16,384]{2,1,0:T(8,128)(2,1)}, u32[]{:S(2)}) copy-start(bf16[64,16,384]{2,1,0:T(8,128)(2,1)} %copy-done.5) | copy-start | bytes 2359300
  110.1 38.1 %copy-start.16 = (bf16[512,512,1]{1,0,2:T(8,128)(2,1)S(1)}, bf16[512,512,1]{1,0,2:T(8,128)(2,1)}, u32[]{:S(2)}) copy-start(bf16[512,512,1]{1,0,2:T(8,128)(2,1)} %constant.117) | copy-start | bytes 1572868
  165.4 6.6 copy-start.10
  165.4 6.6 copy-start.11
  165.4 6.6 copy-start.8
  165.4 6.6 copy-start.9
  165.5 144.0 %all-to-all-start = ((bf16[512,16,384]{2,1,0:T(8,128)(2,1)}), bf16[512,16,384]{2,1,0:T(8,128)(2,1)}, u32[]{:S(2)}, u32[]{:S(2)}) async-start(bf16[512,16,384]{2,1,0:T(8,128)(2,1)} %copy.144), calls=%async_computation | async-start | bytes 12582912 | tf_op jit(solution)/shard_map/all_to_all | solution.py:145
  172.0 141.4 %copy-start.13 = (bf16[1056,1024]{1,0:T(8,128)(2,1)S(1)}, bf16[1056,1024]{1,0:T(8,128)(2,1)}, u32[]{:S(2)}) copy-start(bf16[1056,1024]{1,0:T(8,128)(2,1)} %constant.113) | copy-start | bytes 6488068
  309.4 3.9 copy-start.14
  331.6 12.7 %all-to-all-start.1 = ((f32[32,1,768]{2,1,0:T(1,128)}), f32[32,1,768]{2,1,0:T(1,128)S(1)}, u32[]{:S(2)}, u32[]{:S(2)}) async-start(f32[32,1,768]{2,1,0:T(1,128)} %broadcast_in_dim.116), calls=%async_computation.1 | async-start | bytes 196608 | tf_op jit(solution)/shard_map/all_to_all | solution.py:151
  365.4 153.2 %all-to-all-start.2 = ((bf16[16,512,384]{2,0,1:T(8,128)(2,1)}), bf16[16,512,384]{2,0,1:T(8,128)(2,1)}, u32[]{:S(2)}, u32[]{:S(2)}) async-start(bf16[16,512,384]{2,0,1:T(8,128)(2,1)} %copy.147), calls=%async_computation.2 | async-start | bytes 12582912 | tf_op jit(solution)/shard_map/all_to_all | solution.py:164
  372.3 41.7 %collective-permute-start = (bf16[1,128,512]{2,1,0:T(8,128)(2,1)S(1)}, bf16[1,128,512]{2,1,0:T(8,128)(2,1)S(1)}, u32[]{:S(2)}, u32[]{:S(2)}) collective-permute-start(bf16[1,128,512]{2,1,0:T(8,128)(2,1)S(1)} %get-tuple-element.9), channel_id=1, source_target_pairs={{0,4},{4,8},{8,12},{12,16},{16,20},{20,24},{24,28},{1,5},{5,9},{9,... | collective-permute-start | bytes 393224 | tf_op jit(solution)/shard_map/ppermute | solution.py:68
  375.7 38.6 %collective-permute-start.1 = (bf16[1,128,512]{2,1,0:T(8,128)(2,1)S(1)}, bf16[1,128,512]{2,1,0:T(8,128)(2,1)S(1)}, u32[]{:S(2)}, u32[]{:S(2)}) collective-permute-start(bf16[1,128,512]{2,1,0:T(8,128)(2,1)S(1)} %get-tuple-element.10), channel_id=1, source_target_pairs={{4,0},{8,4},{12,8},{16,12},{20,16},{24,20},{28,24},{5,1},{9,5},{13... | collective-permute-start | bytes 393224 | tf_op jit(solution)/shard_map/ppermute | solution.py:70
  389.4 120.7 %copy-start.2 = (bf16[64,128,512]{2,0,1:T(8,128)(2,1)S(1)}, bf16[64,128,512]{2,0,1:T(8,128)(2,1)}, u32[]{:S(2)}) copy-start(bf16[64,128,512]{2,0,1:T(8,128)(2,1)} %copy.128) | copy-start | bytes 25165828
  415.4 92.6 %collective-permute-start.2 = (bf16[66,1,512]{2,0,1:T(8,128)(2,1)S(1)}, bf16[66,1,512]{2,0,1:T(8,128)(2,1)S(1)}, u32[]{:S(2)}, u32[]{:S(2)}) collective-permute-start(bf16[66,1,512]{2,0,1:T(8,128)(2,1)S(1)} %get-tuple-element.7), channel_id=1, source_target_pairs={{0,1},{1,2},{2,3},{4,5},{5,6},{6,7},{8,9},{9,10},{10,11},{12,13},{... | collective-permute-start | bytes 202760 | tf_op jit(solution)/shard_map/ppermute | solution.py:68
  417.4 92.7 %collective-permute-start.3 = (bf16[66,1,512]{2,0,1:T(8,128)(2,1)S(1)}, bf16[66,1,512]{2,0,1:T(8,128)(2,1)S(1)}, u32[]{:S(2)}, u32[]{:S(2)}) collective-permute-start(bf16[66,1,512]{2,0,1:T(8,128)(2,1)S(1)} %get-tuple-element.8), channel_id=1, source_target_pairs={{1,0},{2,1},{3,2},{5,4},{6,5},{7,6},{9,8},{10,9},{11,10},{13,12},{... | collective-permute-start | bytes 202760 | tf_op jit(solution)/shard_map/ppermute | solution.py:70
  518.7 4.4 copy-start.15
  538.2 95.2 %all-to-all-start.3 = ((bf16[512,16,384]{2,1,0:T(8,128)(2,1)}), bf16[512,16,384]{2,1,0:T(8,128)(2,1)}, u32[]{:S(2)}, u32[]{:S(2)}) async-start(bf16[512,16,384]{2,1,0:T(8,128)(2,1)} %copy.150), calls=%async_computation.3 | async-start | bytes 12582912 | tf_op jit(solution)/shard_map/all_to_all | solution.py:166
  577.3 4.3 copy-start.3
  579.6 2.6 copy-start.12
  579.6 2.6 copy-start.17
  654.7 12.7 %copy-start.4 = (bf16[64,128,128]{2,0,1:T(8,128)(2,1)S(1)}, bf16[64,128,128]{2,0,1:T(8,128)(2,1)}, u32[]{:S(2)}) copy-start(bf16[64,128,128]{2,0,1:T(8,128)(2,1)} %slice_bitcast_fusion.2) | copy-start | bytes 6291460
  667.4 19.3 %copy-start.1 = (bf16[768,768]{1,0:T(8,128)(2,1)S(1)}, bf16[768,768]{1,0:T(8,128)(2,1)}, u32[]{:S(2)}) copy-start(bf16[768,768]{1,0:T(8,128)(2,1)} %param.22) | copy-start | bytes 3538948
